TPU v7x, 128 devices: a whole 4x4x4 slice. The times are simulated.
128 devices in a mesh: pair: 16 (over x_lo, y, core), win: 8 (over x_hi, z).
Axes of the slice: x: 4 (x_hi: 2, x_lo: 2; x = x_hi * 2 + x_lo), y: 4, z: 4, core: 2. Of those that a mesh axis runs over, the one named last changes fastest.
Arguments:
- traces: bfloat16 [4096, 256, 1024], P('pair', 'win'), may hold values from -210 to 210, as said below
- partner: int32 [2, 16], replicated, may hold values from 0 to 15, as said below
- block_ids: int32 [16], replicated, may hold values from 0 to 15, each once
Outputs:
- correlations: float32 [2, 32, 2, 4096, 256], P(None, 'win', None, 'pair')
Inputs may be any that keep to these rules, and one draw needn't show every extreme that they name: traces are noise whose amplitude and spectral colour vary from channel to channel and window to window. Each row of partner pairs every fibre block with one other block: partner[r, partner[r, b]] = b and partner[r, b] != b; the rows are distinct rounds of one round-robin plan. block_ids names each fibre block once.
All inputs are finite; a program needn't handle non-finite values.
Results may differ from a plain program's by a relative error of at most 0.0058.
Values may be sent and summed in bfloat16 or wider, within the bound.
A program may use at most 128 MiB of HBM per device.

v0:
```python
import math

import jax
import jax.numpy as jnp
from jax import lax
from jax.sharding import PartitionSpec as P

SAMPLES = 1024
BINS = 32
FIRST_BIN = 16
BIN_STEP = 8
ROUNDS = 2


def tapered_table():
    sample = jnp.arange(SAMPLES, dtype=jnp.int32)
    freq = FIRST_BIN + BIN_STEP * jnp.arange(BINS, dtype=jnp.int32)
    phase = sample[:, None] * freq[None, :] % SAMPLES
    angle = 2.0 * math.pi / SAMPLES * phase.astype(jnp.float32)
    taper = 0.5 - 0.5 * jnp.cos(2.0 * math.pi / SAMPLES * sample.astype(jnp.float32))
    real_part = taper[:, None] * jnp.cos(angle)
    imag_part = -taper[:, None] * jnp.sin(angle)
    return jnp.concatenate([real_part, imag_part], axis=1).astype(jnp.bfloat16)


def whitened(trace_rows, dft_table):
    raw = jnp.dot(trace_rows, dft_table, preferred_element_type=jnp.float32)
    power = jnp.mean(raw * raw, axis=-1, keepdims=True)
    return (raw * lax.rsqrt(power + 1e-05)).astype(jnp.bfloat16)


def correlate(local_spec, remote):
    rotated = jnp.concatenate([local_spec[1:2], -local_spec[0:1]], axis=0)
    stacked = jnp.stack([local_spec, rotated], axis=0)
    return jnp.einsum("kcbwi,cbwj->bkij", stacked, remote, preferred_element_type=jnp.float32)


def partner_devices(partner_row, block_ids, slots, holder):
    wanted = jnp.sum(
        jnp.where(block_ids[:, None] == slots[None, :], partner_row[None, :], 0), axis=1
    )
    return jnp.sum(jnp.where(wanted[:, None] == slots[None, :], holder[None, :], 0), axis=1)


def spread_spectra(spectra, pair_count):
    return lax.all_to_all(
        spectra.reshape(pair_count, -1), "pair", split_axis=0, concat_axis=0, tiled=True
    )


def local(traces, partner, block_ids):
    dft_table = tapered_table()
    channels_dev, window_devices, samples = traces.shape
    trace_rows = traces.reshape(channels_dev * window_devices, samples)
    flat_spec = whitened(trace_rows, dft_table)
    pair_count = lax.axis_size("pair")
    win_count = lax.axis_size("win")
    stack_scale = 1.0 / math.sqrt(window_devices * win_count)
    spectra = flat_spec.reshape(channels_dev, window_devices, 2, -1).transpose(2, 3, 1, 0)
    spectra = lax.all_to_all(spectra, "win", split_axis=1, concat_axis=2, tiled=True)
    pieces = spread_spectra(spectra, pair_count)
    spec_shape = spectra.shape
    slots = jnp.arange(pair_count, dtype=jnp.int32)
    holder = jnp.sum(jnp.where(block_ids[None, :] == slots[:, None], slots[None, :], 0), axis=1)
    remotes = []
    for round_no in range(ROUNDS):
        targets = partner_devices(partner[round_no], block_ids, slots, holder)
        outgoing = jnp.take(pieces, targets, axis=0)
        arrived = lax.all_to_all(outgoing, "pair", split_axis=0, concat_axis=0, tiled=True)
        remotes.append(arrived.reshape(spec_shape))
    results = []
    for remote in remotes:
        results.append(correlate(spectra, remote) * stack_scale)
    return jnp.stack(results, axis=0)


def solution(mesh):
    placed = (P("pair", "win", None), P(), P())
    return jax.shard_map(
        local,
        mesh=mesh,
        in_specs=placed,
        out_specs=P(None, "win", None, "pair", None),
        check_vma=False,
    )
```

profile of v0, /device:TPU:1, one launch (start us, length us, event | category | flops | bytes accessed | tf_op | source)
XLA Modules:
  0.0 153.8 jit_solution(7546912558513122179)
XLA Ops:
  0.7 11.0 %multiply_reduce_fusion = (f32[8192]{0:T(1024)S(1)}, f32[64,8192]{1,0:T(8,128)S(1)}) fusion(bf16[8192,1024]{1,0:T(8,128)(2,1)} %bitcast.55, bf16[1024,32]{0,1:T(8,128)(2,1)S(1)} %get-tuple-element.16, bf16[1024,32]{0,1:T(8,128)(2,1)S(1)} %get-tuple-element.15), kind=kOutput, calls=%fused_computation.9 | convolution fusion | flops 1075044352 | bytes 19038208 | tf_op jit(solution)/shard_map/dot_general | solution.py:27
  11.8 4.4 %reshape.75 = bf16[256,32,2,32]{1,0,3,2:T(8,128)(2,1)} reshape(bf16[8192,64]{0,1:T(8,128)(2,1)S(1)} %fusion.2) | data formatting | bytes 2097152 | tf_op jit(solution)/shard_map/reshape | solution.py:59
  16.2 3.5 %copy.62 = bf16[2,32,32,256]{3,2,0,1:T(8,128)(2,1)S(1)} copy(bf16[2,32,32,256]{2,3,1,0:T(8,128)(2,1)} %bitcast.54) | data formatting | bytes 2097152 | tf_op jit(solution)/shard_map/transpose | solution.py:59
  19.7 23.8 %all_to_all.46 = bf16[2,32,32,256]{3,2,0,1:T(8,128)(2,1)S(1)} all-to-all(bf16[2,32,32,256]{3,2,0,1:T(8,128)(2,1)S(1)} %copy.62), channel_id=1, replica_groups=mesh['pair'=16,'win'=8] {'win'}, dimensions={1} | all-to-all | bytes 2097152 | tf_op jit(solution)/shard_map/all_to_all | solution.py:60
  43.5 3.1 %all_to_all.41 = bf16[16,1,32768]{2,1,0:T(2,128)(2,1)} reshape(bf16[2,4,8,32,256]{4,3,2,1,0:T(8,128)(2,1)S(1)} %copy.64) | data formatting | bytes 2097152 | tf_op jit(solution)/shard_map/all_to_all | solution.py:46
  47.1 8.3 %reduce.3 = bf16[16,32768]{1,0:T(8,128)(2,1)S(1)} reduce(bf16[16,1,32768]{2,1,0:T(2,128)(2,1)} %all_to_all.41, bf16[]{:T(256)} %broadcast.119), dimensions={1}, to_apply=%all_to_all.41.reduce_sub_computation | reduce | bytes 2097154 | tf_op jit(solution)/shard_map/all_to_all | solution.py:46
  55.4 1.6 %reshape.106 = bf16[16,2,16384]{2,1,0:T(2,128)(2,1)} reshape(bf16[16,32768]{1,0:T(8,128)(2,1)S(1)} %reduce.3) | data formatting | bytes 2097152
  57.0 7.1 %all-to-all-start.1 = ((bf16[16,2,16384]{2,1,0:T(2,128)(2,1)}), bf16[16,2,16384]{2,1,0:T(2,128)(2,1)S(1)}, u32[]{:S(2)}, u32[]{:S(2)}) async-start(bf16[16,2,16384]{2,1,0:T(2,128)(2,1)} %reshape.106), calls=%async_computation.1 | async-start | bytes 2097152 | tf_op jit(solution)/shard_map/all_to_all | solution.py:46
  64.6 15.2 %all-to-all-done.1 = bf16[16,2,16384]{2,1,0:T(2,128)(2,1)S(1)} async-done(((bf16[16,2,16384]{2,1,0:T(2,128)(2,1)}), bf16[16,2,16384]{2,1,0:T(2,128)(2,1)S(1)}, u32[]{:S(2)}, u32[]{:S(2)}) %all-to-all-start.1) | async-done | bytes 1048608 | tf_op jit(solution)/shard_map/all_to_all | solution.py:46
  79.7 3.4 %reshape.107 = bf16[16,1,32768]{2,1,0:T(2,128)(2,1)} reshape(bf16[16,2,16384]{2,1,0:T(2,128)(2,1)S(1)} %all-to-all-done.1) | data formatting | bytes 2097152
  83.2 2.7 %copy.92 = bf16[16,1,32768]{2,0,1:T(8,128)(2,1)S(1)} copy(bf16[16,1,32768]{2,1,0:T(2,128)(2,1)} %reshape.107) | data formatting | bytes 2097152
  85.9 2.2 %gather_fusion.1 = bf16[16,32768]{1,0:T(8,128)(2,1)} fusion(bf16[16,32768]{1,0:T(8,128)(2,1)S(1)} %bitcast.52, s32[1024]{0:T(1024)S(1)} %pad_clamp_fusion), kind=kCustom, calls=%fused_computation.1.clone | custom fusion | bytes 2097216 | tf_op jit(solution)/shard_map/jit(_take)/gather | solution.py:68
  88.1 2.2 %gather_fusion = bf16[16,32768]{1,0:T(8,128)(2,1)} fusion(bf16[16,32768]{1,0:T(8,128)(2,1)S(1)} %bitcast.53, s32[1024]{0:T(1024)S(1)} %pad_clamp_fusion.1), kind=kCustom, calls=%fused_computation.clone | custom fusion | bytes 2097216 | tf_op jit(solution)/shard_map/jit(_take)/gather | solution.py:68
  90.3 1.4 select_bitcast_fusion.1
  91.7 2.0 %reduce.5 = bf16[16,32768]{1,0:T(8,128)(2,1)} reduce(bf16[16,1,32768]{2,0,1:T(8,128)(2,1)S(1)} %select_bitcast_fusion.1, bf16[]{:T(256)} %broadcast.119), dimensions={1}, to_apply=%copy.72.reduce_sub_computation | reduce | bytes 2097154 | tf_op jit(solution)/shard_map/all_to_all | solution.py:69
  93.8 2.7 %reshape.110 = bf16[16,2,16384]{2,1,0:T(2,128)(2,1)} reshape(bf16[16,32768]{1,0:T(8,128)(2,1)} %reduce.5) | data formatting | bytes 2097152
  96.5 5.0 %all-to-all-start.2 = ((bf16[16,2,16384]{2,1,0:T(2,128)(2,1)}), bf16[16,2,16384]{2,1,0:T(2,128)(2,1)}, u32[]{:S(2)}, u32[]{:S(2)}) async-start(bf16[16,2,16384]{2,1,0:T(2,128)(2,1)} %reshape.110), calls=%async_computation.2 | async-start | bytes 2097152 | tf_op jit(solution)/shard_map/all_to_all | solution.py:69
  101.5 1.1 select_bitcast_fusion
  102.7 2.6 %reduce.4 = bf16[16,32768]{1,0:T(8,128)(2,1)S(1)} reduce(bf16[16,1,32768]{2,0,1:T(8,128)(2,1)} %select_bitcast_fusion, bf16[]{:T(256)} %broadcast.119), dimensions={1}, to_apply=%copy.74.reduce_sub_computation | reduce | bytes 2097154 | tf_op jit(solution)/shard_map/all_to_all | solution.py:69
  105.2 1.6 %reshape.108 = bf16[16,2,16384]{2,1,0:T(2,128)(2,1)} reshape(bf16[16,32768]{1,0:T(8,128)(2,1)S(1)} %reduce.4) | data formatting | bytes 2097152
  106.9 10.5 %all-to-all-done.2 = bf16[16,2,16384]{2,1,0:T(2,128)(2,1)} async-done(((bf16[16,2,16384]{2,1,0:T(2,128)(2,1)}), bf16[16,2,16384]{2,1,0:T(2,128)(2,1)}, u32[]{:S(2)}, u32[]{:S(2)}) %all-to-all-start.2) | async-done | bytes 1048608 | tf_op jit(solution)/shard_map/all_to_all | solution.py:69
  117.4 4.4 %all-to-all-start.3 = ((bf16[16,2,16384]{2,1,0:T(2,128)(2,1)}), bf16[16,2,16384]{2,1,0:T(2,128)(2,1)S(1)}, u32[]{:S(2)}, u32[]{:S(2)}) async-start(bf16[16,2,16384]{2,1,0:T(2,128)(2,1)} %reshape.108), calls=%async_computation.3 | async-start | bytes 2097152 | tf_op jit(solution)/shard_map/all_to_all | solution.py:69
  121.8 1.3 copy.69
  123.8 1.1 maximum_bitcast_fusion
  124.9 4.3 %reshape.111 = bf16[16,1,32768]{2,1,0:T(2,128)(2,1)S(1)} reshape(bf16[16,2,16384]{2,1,0:T(2,128)(2,1)} %all-to-all-done.2) | data formatting | bytes 2097152
  129.2 7.4 %reduce.1 = bf16[16,32768]{1,0:T(8,128)(2,1)} reduce(bf16[16,1,32768]{2,1,0:T(2,128)(2,1)S(1)} %reshape.111, bf16[]{:T(256)} %constant.44), dimensions={1}, to_apply=%all_to_all.38.reduce_sub_computation | reduce | bytes 2097154 | tf_op jit(solution)/shard_map/all_to_all | solution.py:69
  136.5 2.3 %reshape.76 = bf16[2,4,256,256]{3,2,1,0:T(8,128)(2,1)} reshape(bf16[16,32768]{1,0:T(8,128)(2,1)} %reduce.1) | data formatting | bytes 2097152 | tf_op jit(solution)/shard_map/reshape | solution.py:70
  138.9 1.3 reshape.109
  140.2 6.4 %reduce.2 = bf16[16,32768]{1,0:T(8,128)(2,1)S(1)} reduce(bf16[16,1,32768]{2,1,0:T(2,128)(2,1)S(1)} %reshape.109, bf16[]{:T(256)} %constant.44), dimensions={1}, to_apply=%all_to_all.40.reduce_sub_computation | reduce | bytes 2097154 | tf_op jit(solution)/shard_map/all_to_all | solution.py:69
  146.6 1.3 reshape.77
  147.9 2.7 %fusion.1 = f32[1,4,2,256,256]{4,3,2,1,0:T(8,128)S(1)} fusion(bf16[1,2,4,256,256]{3,4,1,0,2:T(8,128)(2,1)} %maximum_bitcast_fusion, bf16[1,2,4,256,256]{3,4,1,0,2:T(8,128)(2,1)} %copy.69, bf16[2,4,256,256]{3,2,1,0:T(8,128)(2,1)} %reshape.76), kind=kOutput, calls=%fused_computation.7 | convolution fusion | flops 538443776 | bytes 5242880 | tf_op jit(solution)/shard_map/kcbwi,cbwj->bkij/dot_general | solution.py:35
  151.4 2.4 %pad_maximum_fusion = f32[2,4,2,256,256]{4,3,2,1,0:T(8,128)} fusion(f32[1,4,2,256,256]{4,3,2,1,0:T(8,128)S(1)} %fusion, f32[1,4,2,256,256]{4,3,2,1,0:T(8,128)S(1)} %fusion.1), kind=kLoop, calls=%fused_computation.2 | loop fusion | flops 1048576 | bytes 8388608 | tf_op jit(solution)/shard_map/stack | solution.py:74
  (34 shorter events, 3.2 us)
Async XLA Ops:
  55.4 8.7 %copy-start.5 = (s32[2,16]{1,0:T(2,128)S(1)}, s32[2,16]{1,0:T(2,128)}, u32[]{:S(2)}) copy-start(s32[2,16]{1,0:T(2,128)} %param.6) | copy-start | bytes 388
  55.4 8.7 %copy-start.4 = (s32[16]{0:T(128)S(1)}, s32[16]{0:T(128)}, u32[]{:S(2)}) copy-start(s32[16]{0:T(128)} %param.7) | copy-start | bytes 196
  57.0 22.7 %all-to-all-start.1 = ((bf16[16,2,16384]{2,1,0:T(2,128)(2,1)}), bf16[16,2,16384]{2,1,0:T(2,128)(2,1)S(1)}, u32[]{:S(2)}, u32[]{:S(2)}) async-start(bf16[16,2,16384]{2,1,0:T(2,128)(2,1)} %reshape.106), calls=%async_computation.1 | async-start | bytes 2097152 | tf_op jit(solution)/shard_map/all_to_all | solution.py:46
  93.8 7.8 %copy-start = (bf16[16,32768]{1,0:T(8,128)(2,1)S(1)}, bf16[16,32768]{1,0:T(8,128)(2,1)}, u32[]{:S(2)}) copy-start(bf16[16,32768]{1,0:T(8,128)(2,1)} %gather_fusion.1) | copy-start | bytes 3145732
  96.5 20.9 %all-to-all-start.2 = ((bf16[16,2,16384]{2,1,0:T(2,128)(2,1)}), bf16[16,2,16384]{2,1,0:T(2,128)(2,1)}, u32[]{:S(2)}, u32[]{:S(2)}) async-start(bf16[16,2,16384]{2,1,0:T(2,128)(2,1)} %reshape.110), calls=%async_computation.2 | async-start | bytes 2097152 | tf_op jit(solution)/shard_map/all_to_all | solution.py:69
  117.4 21.5 %all-to-all-start.3 = ((bf16[16,2,16384]{2,1,0:T(2,128)(2,1)}), bf16[16,2,16384]{2,1,0:T(2,128)(2,1)S(1)}, u32[]{:S(2)}, u32[]{:S(2)}) async-start(bf16[16,2,16384]{2,1,0:T(2,128)(2,1)} %reshape.108), calls=%async_computation.3 | async-start | bytes 2097152 | tf_op jit(solution)/shard_map/all_to_all | solution.py:69
  147.9 2.7 %copy-start.1 = (bf16[1,2,4,256,256]{3,4,1,0,2:T(8,128)(2,1)S(1)}, bf16[1,2,4,256,256]{3,4,1,0,2:T(8,128)(2,1)}, u32[]{:S(2)}) copy-start(bf16[1,2,4,256,256]{3,4,1,0,2:T(8,128)(2,1)} %copy.69) | copy-start | bytes 3145732
  147.9 2.7 %copy-start.2 = (bf16[1,2,4,256,256]{3,4,1,0,2:T(8,128)(2,1)S(1)}, bf16[1,2,4,256,256]{3,4,1,0,2:T(8,128)(2,1)}, u32[]{:S(2)}) copy-start(bf16[1,2,4,256,256]{3,4,1,0,2:T(8,128)(2,1)} %maximum_bitcast_fusion) | copy-start | bytes 3145732
  147.9 2.8 %copy-start.3 = (bf16[2,4,256,256]{3,2,1,0:T(8,128)(2,1)S(1)}, bf16[2,4,256,256]{3,2,1,0:T(8,128)(2,1)}, u32[]{:S(2)}) copy-start(bf16[2,4,256,256]{3,2,1,0:T(8,128)(2,1)} %reshape.77) | copy-start | bytes 3145732
where the time goes:
time: 155 us; the launch traced here: 154 us
  local copies, waits for them, and re-layouts  39.3 us (25%)
  other arithmetic  33.9 us (22%)
  waiting for transfers between devices  25.7 us (17%)
  blocking collectives  23.8 us (15%)
  starting transfers between devices  16.5 us (11%)
  matrix products  14.4 us (9%)
    all_to_all x1, blocking collectives, local(): lax.all_to_all(spectra, 'win', split_axis=1, concat_axis=2, tiled=True)  23.8 us
    all_to_all x6, other arithmetic, local(): lax.all_to_all(outgoing, 'pair', split_axis=0, concat_axis=0, tiled=True)  20.9 us
    unnamed x19, local copies, waits for them, and re-layouts  17.8 us
    all_to_all x1, waiting for transfers between devices, spread_spectra(): lax.all_to_all(spectra.reshape(pair_count, -1), 'pair', split_axis=0, con...  15.2 us
    dot_general x1, matrix products, whitened(): raw = jnp.dot(trace_rows, dft_table, preferred_element_type=jnp.float32)  11 us
    all_to_all x2, waiting for transfers between devices, local(): lax.all_to_all(outgoing, 'pair', split_axis=0, concat_axis=0, tiled=True)  10.5 us
    all_to_all x2, starting transfers between devices, local(): lax.all_to_all(outgoing, 'pair', split_axis=0, concat_axis=0, tiled=True)  9.44 us
    all_to_all x1, other arithmetic, spread_spectra(): lax.all_to_all(spectra.reshape(pair_count, -1), 'pair', split_axis=0, con...  8.27 us
  transfers between devices with their start and end apart: 3, of which 2 were waited for; matrix products, arithmetic and copies ran while one was open for 15% of the time, Pallas kernels for 0%

commit v1 on v0

v1 whole, which is shorter than its diff:
```python
import functools
import math

import jax
import jax.numpy as jnp
import numpy as np
from jax import lax
from jax.experimental import pallas as pl
from jax.experimental.pallas import tpu as pltpu
from jax.sharding import PartitionSpec as P

SAMPLES = 1024
BINS = 32
FIRST_BIN = 16
BIN_STEP = 8
ROUNDS = 2
NY = 4
NZ = 4
N_WIN = 2 * NZ
N_COL = NY * 2
BINS_DEV = BINS // N_WIN
PARTS = 2 * BINS_DEV
WCH = 16
CCH = 128
MESH = pl.DeviceIdType.MESH


def dft_columns():
    sample = np.arange(SAMPLES)
    freq = FIRST_BIN + BIN_STEP * np.arange(BINS)
    angle = 2.0 * np.pi / SAMPLES * (sample[:, None] * freq[None, :] % SAMPLES)
    taper = 0.5 - 0.5 * np.cos(2.0 * np.pi / SAMPLES * sample)
    both = np.stack([taper[:, None] * np.cos(angle), -taper[:, None] * np.sin(angle)], axis=2)
    return jnp.asarray(both.reshape(SAMPLES, 2 * BINS).astype(np.float32), dtype=jnp.bfloat16)


def spread_kernel(
    x_hbm, table, partner, block_ids, lhs_out, rem_out,
    raw, ybuf, lhs, targets,
    xsem, s1, r1, s2, r2, s3, r3, s4, r4, l4, lsem, *buffers,
):
    pair = lax.axis_index("pair")
    win = lax.axis_index("win")
    xlo, col = pair // N_COL, pair % N_COL
    y, core = col // 2, col % 2
    xhi, z = win // NZ, win % NZ
    chunks = len(buffers) // 5
    xbufs, sends, owns, mids, sbufs = (buffers[i * chunks : (i + 1) * chunks] for i in range(5))
    halves = lhs.shape[3] // (2 * N_WIN * WCH)

    def x_copy(g):
        h, v = g // halves, g % halves
        return pltpu.make_async_copy(
            x_hbm.at[pl.ds(h * CCH, CCH), pl.ds(v * WCH, WCH)], xbufs[g], xsem.at[g]
        )

    for g in range(chunks):
        x_copy(g).start()

    win_peers = [((xhi + a) % 2) * NZ + (z + b) % NZ for a in range(2) for b in range(NZ)][1:]
    col_peers = [((y + a) % NY) * 2 + (core + b) % 2 for a in range(NY) for b in range(2)][1:]
    mirror = ((1 - xlo) * N_COL + col, win)

    barrier = pltpu.get_barrier_semaphore()
    for peer in win_peers:
        pl.semaphore_signal(barrier, inc=1, device_id=(pair, peer), device_id_type=MESH)
    for peer in col_peers:
        pl.semaphore_signal(barrier, inc=1, device_id=(xlo * N_COL + peer, win), device_id_type=MESH)
    pl.semaphore_signal(barrier, inc=1, device_id=mirror, device_id_type=MESH)

    @pl.loop(0, ROUNDS)
    def _(r):
        @pl.loop(0, N_COL)
        def _(d):
            wanted = partner[r, block_ids[xlo * N_COL + d]]

            def look(q, found):
                return jnp.where(block_ids[q] == wanted, q, found)

            targets[r, d] = lax.fori_loop(0, 2 * N_COL, look, jnp.int32(0))

    def remote(src, dst, send, recv, device):
        return pltpu.make_async_remote_copy(
            src_ref=src, dst_ref=dst, send_sem=send, recv_sem=recv, device_id=device, device_id_type=MESH
        )

    def transform(g):
        x_copy(g).wait()
        rows = min(512, CCH * WCH)

        @pl.loop(0, CCH * WCH // rows)
        def _(i):
            block = xbufs[g][pl.ds(i * (rows // WCH), rows // WCH)].reshape(rows, SAMPLES)
            raw[pl.ds(i * rows, rows), :] = jnp.dot(block, table[...], preferred_element_type=jnp.float32)

        @pl.loop(0, WCH)
        def _(w):
            part = raw[pl.ds(w, CCH, stride=WCH), :].T[: 2 * BINS]
            power = jnp.sum(part * part, axis=0, keepdims=True) * (1.0 / (2 * BINS))
            ybuf[pl.ds(w, 2 * BINS, stride=WCH), :] = part * lax.rsqrt(power + 1e-05)

        sends[g][...] = ybuf[...].astype(jnp.bfloat16).reshape(N_WIN, PARTS, WCH, CCH)

    def phase1(g):
        for peer in win_peers:
            remote(sends[g].at[peer], owns[g].at[win], s1.at[g], r1.at[g, win], (pair, peer)).start()
        owns[g][win] = sends[g][win]

    def phase2(g):
        for peer in win_peers:
            remote(sends[g].at[peer], owns[g].at[peer], s1.at[g], r1.at[g, peer], (pair, peer)).wait_recv()
        for peer in col_peers:
            remote(
                owns[g].at[peer], mids[g].at[pair], s2.at[g], r2.at[g, col], (xlo * N_COL + peer, win)
            ).start()
        mids[g][pair] = owns[g][col]

    def phase3(g):
        remote(mids[g].at[pair], mids[g].at[pair], s3.at[g], r3.at[g], mirror).start()
        for peer in col_peers:
            slot = xlo * N_COL + peer
            remote(owns[g].at[peer], mids[g].at[slot], s2.at[g], r2.at[g, peer], (slot, win)).wait_recv()
            remote(mids[g].at[slot], mids[g].at[slot], s3.at[g], r3.at[g], mirror).start()

    def phase4(g):
        theirs = mids[g].at[pl.ds((1 - xlo) * N_COL, N_COL)]
        remote(theirs, theirs, s3.at[g], r3.at[g], mirror).wait_recv()
        for peer in [*col_peers, col]:
            for r in range(ROUNDS):
                sbufs[g][peer, r] = mids[g][targets[r, peer]]
            if peer is col:
                pltpu.make_async_copy(sbufs[g].at[col], rem_out.at[g, col], l4.at[g]).start()
            else:
                remote(
                    sbufs[g].at[peer], rem_out.at[g, col], s4.at[g], r4.at[g], (xlo * N_COL + peer, win)
                ).start()

    def left_side(g):
        h, v = g // halves, g % halves
        rows = pl.ds(h * CCH, CCH)
        span = N_WIN * WCH
        for k in range(BINS_DEV):
            for c in range(2):
                part = owns[g][:, 2 * k + c].reshape(span, CCH).astype(jnp.float32).T
                plain = part.astype(jnp.bfloat16)
                turned = (part if c else -part).astype(jnp.bfloat16)
                lhs[k, 0, rows, pl.ds((c * halves + v) * span, span)] = plain
                lhs[k, 1, rows, pl.ds(((1 - c) * halves + v) * span, span)] = turned

    transform(0)
    pl.semaphore_wait(barrier, len(win_peers) + len(col_peers) + 1)
    phase1(0)
    transform(1)
    phase1(1)
    phase2(0)
    transform(2)
    phase1(2)
    phase3(0)
    phase2(1)
    transform(3)
    phase1(3)
    phase4(0)
    phase3(1)
    phase2(2)
    left_side(0)
    phase2(3)
    left_side(1)
    phase4(1)
    phase3(2)
    left_side(2)
    phase3(3)
    left_side(3)
    lhs_copy = pltpu.make_async_copy(lhs, lhs_out, lsem)
    lhs_copy.start()
    phase4(2)
    phase4(3)

    lhs_copy.wait()
    for g in range(chunks):
        seven = owns[g].at[pl.ds(0, N_WIN - 1)]
        eight = mids[g].at[pl.ds(0, N_COL)]
        rounds = sbufs[g].at[pl.ds(0, N_COL - 1)]
        landed = rem_out.at[g, pl.ds(0, N_COL - 1)]
        remote(seven, seven, s1.at[g], r1.at[g, 0], mirror).wait_send()
        remote(seven, seven, s2.at[g], r2.at[g, 0], mirror).wait_send()
        remote(eight, eight, s3.at[g], r3.at[g], mirror).wait_send()
        remote(rounds, landed, s4.at[g], r4.at[g], mirror).wait_send()
        pltpu.make_async_copy(sbufs[g].at[col], rem_out.at[g, col], l4.at[g]).wait()
        remote(rounds, landed, s4.at[g], r4.at[g], mirror).wait_recv()


def spread(traces, partner, block_ids):
    channels, windows, _ = traces.shape
    chans, halves = channels // CCH, windows // WCH
    chunks = chans * halves
    piece = (PARTS, WCH, CCH)
    bf16 = jnp.bfloat16
    lhs_shape = (BINS_DEV, 2, channels, 2 * N_WIN * windows)
    rem_shape = (chunks, N_COL, ROUNDS, *piece)
    dma = pltpu.SemaphoreType.DMA
    table = jnp.pad(dft_columns(), ((0, 0), (0, 128 - 2 * BINS)))
    return pl.pallas_call(
        spread_kernel,
        out_shape=(jax.ShapeDtypeStruct(lhs_shape, bf16), jax.ShapeDtypeStruct(rem_shape, bf16)),
        in_specs=[
            pl.BlockSpec(memory_space=pl.ANY),
            pl.BlockSpec(memory_space=pltpu.VMEM),
            pl.BlockSpec(memory_space=pltpu.SMEM),
            pl.BlockSpec(memory_space=pltpu.SMEM),
        ],
        out_specs=(pl.BlockSpec(memory_space=pl.ANY), pl.BlockSpec(memory_space=pl.ANY)),
        scratch_shapes=[
            pltpu.VMEM((CCH * WCH, 128), jnp.float32),
            pltpu.VMEM((2 * BINS * WCH, CCH), jnp.float32),
            pltpu.VMEM(lhs_shape, bf16),
            pltpu.SMEM((ROUNDS, N_COL), jnp.int32),
            dma((chunks,)),
            dma((chunks,)), dma((chunks, N_WIN)),
            dma((chunks,)), dma((chunks, N_COL)),
            dma((chunks,)), dma((chunks,)),
            dma((chunks,)), dma((chunks,)),
            dma((chunks,)),
            dma,
            *[pltpu.VMEM((CCH, WCH, SAMPLES), bf16)] * chunks,
            *[pltpu.VMEM((N_WIN, *piece), bf16)] * (2 * chunks),
            *[pltpu.VMEM((2 * N_COL, *piece), bf16)] * chunks,
            *[pltpu.VMEM((N_COL, ROUNDS, *piece), bf16)] * chunks,
        ],
        compiler_params=pltpu.CompilerParams(
            collective_id=0, has_side_effects=True, vmem_limit_bytes=50 * 1024 * 1024
        ),
        name="spread",
    )(traces, table, partner, block_ids)


def correlate_kernel(scale, lhs, rem, out):
    chunks, n_win = rem.shape[:2]
    channels = lhs.shape[2]
    chans = channels // CCH
    halves = chunks // chans
    columns = []
    for h in range(chans):
        rows = [
            rem[h * halves + v, :, 0, c].reshape(n_win * WCH, CCH) for c in range(2) for v in range(halves)
        ]
        columns.append(jnp.concatenate(rows, axis=0))
    right = jnp.concatenate(columns, axis=1)
    left = lhs[0].reshape(2 * channels, lhs.shape[3])
    result = jnp.dot(left, right, preferred_element_type=jnp.float32) * scale
    out[0, 0] = result.reshape(out.shape[2:])


def correlate(lhs, rem, scale):
    chunks, n_win = rem.shape[:2]
    bins, _, channels, depth = lhs.shape
    out_shape = (ROUNDS, bins, 2, channels, channels)
    return pl.pallas_call(
        functools.partial(correlate_kernel, scale),
        grid=(bins, ROUNDS),
        out_shape=jax.ShapeDtypeStruct(out_shape, jnp.float32),
        in_specs=[
            pl.BlockSpec((1, 2, channels, depth), lambda k, r: (k, 0, 0, 0)),
            pl.BlockSpec((chunks, n_win, 1, 2, WCH, CCH), lambda k, r: (0, 0, r, k, 0, 0)),
        ],
        out_specs=pl.BlockSpec((1, 1, 2, channels, channels), lambda k, r: (r, k, 0, 0, 0)),
        name="correlate",
    )(lhs, rem)


def local(traces, partner, block_ids):
    windows = traces.shape[1] * N_WIN
    lhs, rem = spread(traces, partner, block_ids)
    return correlate(lhs, rem, 1.0 / math.sqrt(windows))


def solution(mesh):
    placed = (P("pair", "win", None), P(), P())
    return jax.shard_map(
        local,
        mesh=mesh,
        in_specs=placed,
        out_specs=P(None, "win", None, "pair", None),
        check_vma=False,
    )
```

time: 155 us -> 75.4 us (0.49)
  Pallas kernels: 0 us -> 71.5 us
  local copies, waits for them, and re-layouts: 39.3 us -> 3.58 us
  other arithmetic: 33.9 us -> 0 us
  waiting for transfers between devices: 25.7 us -> 0 us
  blocking collectives: 23.8 us -> 0 us
  starting transfers between devices: 16.5 us -> 0 us
  matrix products: 14.4 us -> 0 us
    pallas_call x0 -> x2, Pallas kernels: none -> 71.5 us  [the longest x1 63.5 us: spread(): pl.pallas_call(spread_kernel, out_shape=(jax.ShapeDtypeStruct(lhs_shape,...]
    all_to_all x7 -> x0, other arithmetic: 29.1 us -> none  [the longest x6 20.9 us: local(): lax.all_to_all(outgoing, 'pair', split_axis=0, concat_axis=0, tiled=True)]
    all_to_all x3 -> x0, waiting for transfers between devices: 25.7 us -> none  [the longest x1 15.2 us: spread_spectra(): lax.all_to_all(spectra.reshape(pair_count, -1), 'pair', split_axis=0, con...]
    all_to_all x1 -> x0, blocking collectives: 23.8 us -> none  [local(): lax.all_to_all(spectra, 'win', split_axis=1, concat_axis=2, tiled=True)]
    all_to_all x3 -> x0, starting transfers between devices: 16.5 us -> none  [the longest x2 9.44 us: local(): lax.all_to_all(outgoing, 'pair', split_axis=0, concat_axis=0, tiled=True)]
    dot_general x3 -> x0, matrix products: 14.4 us -> none  [the longest x1 11 us: whitened(): raw = jnp.dot(trace_rows, dft_table, preferred_element_type=jnp.float32)]
    unnamed x19 -> x8, local copies, waits for them, and re-layouts: 17.8 us -> 3.58 us
    reshape x3 -> x0, local copies, waits for them, and re-layouts: 8.05 us -> none  [the longest x1 4.37 us: local(): flat_spec.reshape(channels_dev, window_devices, 2, -1).transpose(2, 3, 1, 0)]
  transfers between devices with their start and end apart: 3 -> 0, of which waited for: 2 -> 0; matrix products, arithmetic and copies ran while one was open for 15% -> 0% of each run, Pallas kernels for 0% -> 0%
where the time goes in v1:
time: 75.4 us; the launch traced here: 75.1 us
  Pallas kernels  71.5 us (95%)
  local copies, waits for them, and re-layouts  3.58 us (5%)
    pallas_call x1, Pallas kernels, spread(): pl.pallas_call(spread_kernel, out_shape=(jax.ShapeDtypeStruct(lhs_shape,...  63.5 us
    pallas_call x1, Pallas kernels, correlate(): pl.pallas_call(functools.partial(correlate_kernel, scale), grid=(bins, RO...  7.94 us
    unnamed x8, local copies, waits for them, and re-layouts  3.58 us

profile of v1, /device:TPU:1, one launch (start us, length us, event | category | flops | bytes accessed | tf_op | source)
XLA Modules:
  0.0 75.1 jit_solution(1727853169148500886)
XLA Ops:
  0.0 0.0 copy-start.1
  0.0 0.9 %copy-done.1 = bf16[1024,128]{1,0:T(8,128)(2,1)S(1)} copy-done((bf16[1024,128]{1,0:T(8,128)(2,1)S(1)}, bf16[1024,128]{1,0:T(8,128)(2,1)}, u32[]{:S(2)}) %copy-start.1) | copy-done | bytes 262168
  1.0 0.0 copy-start.2
  1.0 0.7 copy-done.2
  1.6 0.0 copy-start.3
  1.6 0.7 copy-done.3
  2.3 63.5 %spread.1 = (bf16[4,2,256,512]{3,2,1,0:T(8,128)(2,1)S(1)}, bf16[4,8,2,8,16,128]{5,4,3,2,1,0:T(8,128)(2,1)}) custom-call(bf16[256,32,1024]{2,1,0:T(8,128)(2,1)} %x_hbm.1, bf16[1024,128]{1,0:T(8,128)(2,1)S(1)} %copy-done.1, s32[2,16]{1,0:T(2,128)S(1)} %copy-done.2, s32[16]{0:T(128)S(1)} %copy-done.3), custom_call_target="tpu_custom_call" | custom-call | tf_op jit(solution)/shard_map/spread/pallas_call | solution.py:202
  65.8 0.0 copy-start
  65.8 1.3 %copy-done = bf16[4,2,256,512]{3,2,1,0:T(8,128)(2,1)} copy-done((bf16[4,2,256,512]{3,2,1,0:T(8,128)(2,1)}, bf16[4,2,256,512]{3,2,1,0:T(8,128)(2,1)S(1)}, u32[]{:S(2)}) %copy-start) | copy-done | bytes 2097176
  67.1 7.9 %correlate.1 = f32[2,4,2,256,256]{4,3,2,1,0:T(8,128)} custom-call(bf16[4,2,256,512]{3,2,1,0:T(8,128)(2,1)} %copy-done, bf16[4,8,2,8,16,128]{5,4,3,2,1,0:T(8,128)(2,1)} %get-tuple-element.8.rem), custom_call_target="tpu_custom_call" | custom-call | tf_op jit(solution)/shard_map/correlate/pallas_call | solution.py:257
Async XLA Ops:
  0.0 0.9 %copy-start.1 = (bf16[1024,128]{1,0:T(8,128)(2,1)S(1)}, bf16[1024,128]{1,0:T(8,128)(2,1)}, u32[]{:S(2)}) copy-start(bf16[1024,128]{1,0:T(8,128)(2,1)} %constant.8.table) | copy-start | bytes 786436
  1.0 0.7 copy-start.2
  1.6 0.7 copy-start.3
  65.8 1.3 %copy-start = (bf16[4,2,256,512]{3,2,1,0:T(8,128)(2,1)}, bf16[4,2,256,512]{3,2,1,0:T(8,128)(2,1)S(1)}, u32[]{:S(2)}) copy-start(bf16[4,2,256,512]{3,2,1,0:T(8,128)(2,1)S(1)} %get-tuple-element.7.lhs) | copy-start | bytes 6291460

commit v2 on v1

v2 whole, which is shorter than its diff:
```python
import functools
import math

import jax
import jax.numpy as jnp
import numpy as np
from jax import lax
from jax.experimental import pallas as pl
from jax.experimental.pallas import tpu as pltpu
from jax.sharding import PartitionSpec as P

SAMPLES = 1024
BINS = 32
FIRST_BIN = 16
BIN_STEP = 8
ROUNDS = 2
NY = 4
NZ = 4
N_WIN = 2 * NZ
N_COL = NY * 2
BINS_DEV = BINS // N_WIN
PARTS = 2 * BINS_DEV
WCH = 8
JOIN = 2
LAGS = (2, 4, 6)
CCH = 128
MESH = pl.DeviceIdType.MESH


def dft_columns():
    sample = np.arange(SAMPLES)
    freq = FIRST_BIN + BIN_STEP * np.arange(BINS)
    angle = 2.0 * np.pi / SAMPLES * (sample[:, None] * freq[None, :] % SAMPLES)
    taper = 0.5 - 0.5 * np.cos(2.0 * np.pi / SAMPLES * sample)
    both = np.stack([taper[:, None] * np.cos(angle), -taper[:, None] * np.sin(angle)], axis=2)
    return jnp.asarray(both.reshape(SAMPLES, 2 * BINS).astype(np.float32), dtype=jnp.bfloat16)


def spread_kernel(
    x_hbm, table_hbm, partner_hbm, ids_hbm, lhs_out, rem_out,
    table, partner, block_ids, raw0, raw1, ybuf, lhs, targets,
    xsem, tsem, s1, r1, s2, r2, s3, r3, s4, r4, l4, lsem, *buffers,
):
    pair = lax.axis_index("pair")
    win = lax.axis_index("win")
    xlo, col = pair // N_COL, pair % N_COL
    y, core = col // 2, col % 2
    xhi, z = win // NZ, win % NZ
    chunks = len(buffers) // 5
    xbufs, sends, owns, mids, sbufs = (buffers[i * chunks : (i + 1) * chunks] for i in range(5))
    raws = (raw0, raw1)
    parts_v = lhs.shape[3] // (2 * N_WIN * WCH)

    win_peers = [((xhi + a) % 2) * NZ + (z + b) % NZ for a in range(2) for b in range(NZ)][1:]
    col_peers = [((y + a) % NY) * 2 + (core + b) % 2 for a in range(NY) for b in range(2)][1:]
    mirror = ((1 - xlo) * N_COL + col, win)

    def x_copy(g):
        h, v = g // parts_v, g % parts_v
        return pltpu.make_async_copy(
            x_hbm.at[pl.ds(h * CCH, CCH), pl.ds(v * WCH, WCH)], xbufs[g], xsem.at[g]
        )

    table_copy = pltpu.make_async_copy(table_hbm, table, tsem.at[0])
    partner_copy = pltpu.make_async_copy(partner_hbm, partner, tsem.at[1])
    ids_copy = pltpu.make_async_copy(ids_hbm, block_ids, tsem.at[2])
    table_copy.start()
    for g in range(chunks):
        x_copy(g).start()
    partner_copy.start()
    ids_copy.start()

    barrier = pltpu.get_barrier_semaphore()
    for peer in win_peers:
        pl.semaphore_signal(barrier, inc=1, device_id=(pair, peer), device_id_type=MESH)
    for peer in col_peers:
        pl.semaphore_signal(barrier, inc=1, device_id=(xlo * N_COL + peer, win), device_id_type=MESH)
    pl.semaphore_signal(barrier, inc=1, device_id=mirror, device_id_type=MESH)

    def find_targets():
        partner_copy.wait()
        ids_copy.wait()

        @pl.loop(0, ROUNDS)
        def _(r):
            @pl.loop(0, N_COL)
            def _(d):
                wanted = partner[r, block_ids[xlo * N_COL + d]]
                found = jnp.int32(0)
                for q in range(2 * N_COL):
                    found = jnp.where(block_ids[q] == wanted, q, found)
                targets[r, d] = found

    def remote(src, dst, send, recv, device):
        return pltpu.make_async_remote_copy(
            src_ref=src, dst_ref=dst, send_sem=send, recv_sem=recv, device_id=device, device_id_type=MESH
        )

    blocks = 4
    rows = CCH * WCH // blocks

    def product(g, i):
        block = xbufs[g][pl.ds(i * (rows // WCH), rows // WCH)].reshape(rows, SAMPLES)
        raws[g % 2][pl.ds(i * rows, rows), :] = jnp.dot(block, table[...], preferred_element_type=jnp.float32)

    def whiten(g, w):
        part = raws[g % 2][pl.ds(w, CCH, stride=WCH), :].T[: 2 * BINS]
        power = jnp.sum(part * part, axis=0, keepdims=True) * (1.0 / (2 * BINS))
        ybuf[pl.ds(w, 2 * BINS, stride=WCH), :] = part * lax.rsqrt(power + 1e-05)

    def load(g):
        x_copy(g).wait()

    def product_all(g):
        load(g)

        @pl.loop(0, blocks)
        def _(i):
            product(g, i)

    def whiten_all(g):
        for w in range(WCH):
            whiten(g, w)

    def both(g):
        load(g + 1)

        @pl.loop(0, blocks)
        def _(i):
            product(g + 1, i)
            for w in range(WCH // blocks):
                whiten(g, i * (WCH // blocks) + w)

    def transform(g):
        if g == 0:
            table_copy.wait()
            product_all(0)
            whiten_all(0)
        elif g == chunks - 1:
            whiten_all(g)
        else:
            if g == 1:
                product_all(1)
            both(g)
        sends[g][...] = ybuf[...].astype(jnp.bfloat16).reshape(N_WIN, PARTS, WCH, CCH)

    def phase1(g):
        for peer in win_peers:
            remote(sends[g].at[peer], owns[g].at[win], s1.at[g], r1.at[g, win], (pair, peer)).start()
        owns[g][win] = sends[g][win]

    def phase2(g):
        for peer in win_peers:
            remote(sends[g].at[peer], owns[g].at[peer], s1.at[g], r1.at[g, peer], (pair, peer)).wait_recv()
        for peer in col_peers:
            remote(
                owns[g].at[peer], mids[g].at[pair], s2.at[g], r2.at[g, col], (xlo * N_COL + peer, win)
            ).start()
        mids[g][pair] = owns[g][col]

    def phase3(g):
        remote(mids[g].at[pair], mids[g].at[pair], s3.at[g], r3.at[g], mirror).start()
        for peer in col_peers:
            slot = xlo * N_COL + peer
            remote(owns[g].at[peer], mids[g].at[slot], s2.at[g], r2.at[g, peer], (slot, win)).wait_recv()
            remote(mids[g].at[slot], mids[g].at[slot], s3.at[g], r3.at[g], mirror).start()

    def phase4(g):
        theirs = mids[g].at[pl.ds((1 - xlo) * N_COL, N_COL)]
        remote(theirs, theirs, s3.at[g], r3.at[g], mirror).wait_recv()
        for peer in [*col_peers, col]:
            for r in range(ROUNDS):
                sbufs[g][peer, r] = mids[g][targets[r, peer]]
            if peer is col:
                pltpu.make_async_copy(sbufs[g].at[col], rem_out.at[g, col], l4.at[g]).start()
            else:
                remote(
                    sbufs[g].at[peer], rem_out.at[g, col], s4.at[g], r4.at[g], (xlo * N_COL + peer, win)
                ).start()

    def left_side(g):
        h, v = g // parts_v, g % parts_v
        to = pl.ds(h * CCH, CCH)
        span = N_WIN * WCH
        for k in range(BINS_DEV):
            for c in range(2):
                part = jnp.concatenate(
                    [owns[g + j][:, 2 * k + c].reshape(span, CCH).astype(jnp.float32) for j in range(JOIN)], axis=0
                ).T
                plain = part.astype(jnp.bfloat16)
                turned = (part if c else -part).astype(jnp.bfloat16)
                lhs[k, 0, to, pl.ds((c * parts_v + v) * span, JOIN * span)] = plain
                lhs[k, 1, to, pl.ds(((1 - c) * parts_v + v) * span, JOIN * span)] = turned

    lag2, lag3, lag4 = LAGS
    lhs_copy = pltpu.make_async_copy(lhs, lhs_out, lsem)
    for t in range(chunks + lag4):
        if t < chunks:
            transform(t)
            if t == 0:
                pl.semaphore_wait(barrier, len(win_peers) + len(col_peers) + 1)
            phase1(t)
            if t == 0:
                find_targets()
        if 0 <= t - lag2 < chunks:
            phase2(t - lag2)
        if 0 <= t - lag3 < chunks:
            phase3(t - lag3)
        g = t - lag3 - JOIN + 1
        if 0 <= g < chunks and g % JOIN == 0:
            left_side(g)
            if g == chunks - JOIN:
                lhs_copy.start()
        if 0 <= t - lag4 < chunks:
            phase4(t - lag4)

    lhs_copy.wait()
    for g in range(chunks):
        seven = owns[g].at[pl.ds(0, N_WIN - 1)]
        eight = mids[g].at[pl.ds(0, N_COL)]
        rounds = sbufs[g].at[pl.ds(0, N_COL - 1)]
        landed = rem_out.at[g, pl.ds(0, N_COL - 1)]
        remote(seven, seven, s1.at[g], r1.at[g, 0], mirror).wait_send()
        remote(seven, seven, s2.at[g], r2.at[g, 0], mirror).wait_send()
        remote(eight, eight, s3.at[g], r3.at[g], mirror).wait_send()
        remote(rounds, landed, s4.at[g], r4.at[g], mirror).wait_send()
        pltpu.make_async_copy(sbufs[g].at[col], rem_out.at[g, col], l4.at[g]).wait()
        remote(rounds, landed, s4.at[g], r4.at[g], mirror).wait_recv()


def spread(traces, partner, block_ids):
    channels, windows, _ = traces.shape
    chunks = (channels // CCH) * (windows // WCH)
    piece = (PARTS, WCH, CCH)
    bf16, f32 = jnp.bfloat16, jnp.float32
    lhs_shape = (BINS_DEV, 2, channels, 2 * N_WIN * windows)
    rem_shape = (chunks, N_COL, ROUNDS, *piece)
    dma = pltpu.SemaphoreType.DMA
    table = jnp.pad(dft_columns(), ((0, 0), (0, 128 - 2 * BINS)))
    return pl.pallas_call(
        spread_kernel,
        out_shape=(jax.ShapeDtypeStruct(lhs_shape, bf16), jax.ShapeDtypeStruct(rem_shape, bf16)),
        in_specs=[pl.BlockSpec(memory_space=pltpu.HBM)] * 4,
        out_specs=(pl.BlockSpec(memory_space=pl.ANY), pl.BlockSpec(memory_space=pl.ANY)),
        scratch_shapes=[
            pltpu.VMEM(table.shape, bf16),
            pltpu.SMEM(partner.shape, jnp.int32),
            pltpu.SMEM(block_ids.shape, jnp.int32),
            pltpu.VMEM((CCH * WCH, 128), f32),
            pltpu.VMEM((CCH * WCH, 128), f32),
            pltpu.VMEM((2 * BINS * WCH, CCH), f32),
            pltpu.VMEM(lhs_shape, bf16),
            pltpu.SMEM((ROUNDS, N_COL), jnp.int32),
            dma((chunks,)), dma((3,)),
            dma((chunks,)), dma((chunks, N_WIN)),
            dma((chunks,)), dma((chunks, N_COL)),
            dma((chunks,)), dma((chunks,)),
            dma((chunks,)), dma((chunks,)),
            dma((chunks,)),
            dma,
            *[pltpu.VMEM((CCH, WCH, SAMPLES), bf16)] * chunks,
            *[pltpu.VMEM((N_WIN, *piece), bf16)] * (2 * chunks),
            *[pltpu.VMEM((2 * N_COL, *piece), bf16)] * chunks,
            *[pltpu.VMEM((N_COL, ROUNDS, *piece), bf16)] * chunks,
        ],
        compiler_params=pltpu.CompilerParams(
            collective_id=0, has_side_effects=True, vmem_limit_bytes=44 * 1024 * 1024
        ),
        name="spread",
    )(*(pltpu.with_memory_space_constraint(a, pltpu.HBM) for a in (traces, table, partner, block_ids)))


def correlate_kernel(scale, lhs, rem, out):
    k, r = pl.program_id(0), pl.program_id(1)
    chunks, n_win = rem.shape[:2]
    channels = lhs.shape[2]
    chans = channels // CCH
    parts_v = chunks // chans
    columns = []
    for h in range(chans):
        rows = [
            rem[h * parts_v + v, :, r, 2 * k + c].reshape(n_win * WCH, CCH)
            for c in range(2)
            for v in range(parts_v)
        ]
        columns.append(jnp.concatenate(rows, axis=0))
    right = jnp.concatenate(columns, axis=1)
    for t in range(2):
        out[0, 0, t] = jnp.dot(lhs[k, t], right, preferred_element_type=jnp.float32) * scale


def correlate(lhs, rem, scale):
    bins, _, channels, _ = lhs.shape
    out_shape = (ROUNDS, bins, 2, channels, channels)
    return pl.pallas_call(
        functools.partial(correlate_kernel, scale),
        grid=(bins, ROUNDS),
        out_shape=jax.ShapeDtypeStruct(out_shape, jnp.float32),
        in_specs=[pl.BlockSpec(memory_space=pltpu.VMEM)] * 2,
        out_specs=pl.BlockSpec((1, 1, 2, channels, channels), lambda k, r: (r, k, 0, 0, 0)),
        compiler_params=pltpu.CompilerParams(vmem_limit_bytes=16 * 1024 * 1024),
        name="correlate",
    )(lhs, rem)


def local(traces, partner, block_ids):
    windows = traces.shape[1] * N_WIN
    lhs, rem = spread(traces, partner, block_ids)
    return correlate(lhs, rem, 1.0 / math.sqrt(windows))


def solution(mesh):
    placed = (P("pair", "win", None), P(), P())
    return jax.shard_map(
        local,
        mesh=mesh,
        in_specs=placed,
        out_specs=P(None, "win", None, "pair", None),
        check_vma=False,
    )
```

time: 75.4 us -> 62 us (0.82)
  Pallas kernels: 71.5 us -> 61.9 us
  local copies, waits for them, and re-layouts: 3.58 us -> 0 us
    pallas_call x1, Pallas kernels: 63.5 us -> 57.1 us  [spread(): pl.pallas_call(spread_kernel, out_shape=(jax.ShapeDtypeStruct(lhs_shape,...]
    unnamed x8 -> x0, local copies, waits for them, and re-layouts: 3.58 us -> none
    pallas_call x1, Pallas kernels: 7.94 us -> 4.75 us  [correlate(): pl.pallas_call(functools.partial(correlate_kernel, scale), grid=(bins, RO...]
where the time goes in v2:
time: 62 us; the launch traced here: 61.9 us
  Pallas kernels  61.9 us (100%)
    pallas_call x1, Pallas kernels, spread(): pl.pallas_call(spread_kernel, out_shape=(jax.ShapeDtypeStruct(lhs_shape,...  57.1 us
    pallas_call x1, Pallas kernels, correlate(): pl.pallas_call(functools.partial(correlate_kernel, scale), grid=(bins, RO...  4.75 us

profile of v2, /device:TPU:1, one launch (start us, length us, event | category | flops | bytes accessed | tf_op | source)
XLA Modules:
  0.0 61.9 jit_solution(9901472827531940371)
XLA Ops:
  0.0 57.1 %spread.1 = (bf16[4,2,256,512]{3,2,1,0:T(8,128)(2,1)S(1)}, bf16[8,8,2,8,8,128]{5,4,3,2,1,0:T(8,128)(2,1)S(1)}) custom-call(bf16[256,32,1024]{2,1,0:T(8,128)(2,1)} %x_hbm.1, bf16[1024,128]{1,0:T(8,128)(2,1)} %constant.8.table_hbm, s32[2,16]{1,0:T(2,128)} %partner_hbm.1, s32[16]{0:T(128)} %ids_hbm.1), custom_call_target="tpu_custom_call" | custom-call | tf_op jit(solution)/shard_map/spread/pallas_call | solution.py:240
  57.2 4.7 %correlate.1 = f32[2,4,2,256,256]{4,3,2,1,0:T(8,128)} custom-call(bf16[4,2,256,512]{3,2,1,0:T(8,128)(2,1)S(1)} %get-tuple-element.7.lhs, bf16[8,8,2,8,8,128]{5,4,3,2,1,0:T(8,128)(2,1)S(1)} %get-tuple-element.8.rem), custom_call_target="tpu_custom_call" | custom-call | tf_op jit(solution)/shard_map/correlate/pallas_call | solution.py:295

commit v3 on v2

--- a/solution.py
+++ b/solution.py
@@ -19,10 +19,13 @@
 N_WIN = 2 * NZ
 N_COL = NY * 2
 BINS_DEV = BINS // N_WIN
+COL_STEPS = ((2, 0), (1, 0), (3, 0), (2, 1), (1, 1), (3, 1), (0, 1))
+WIN_STEPS = ((1, 2), (1, 1), (1, 3), (0, 2), (1, 0), (0, 1), (0, 3))
 PARTS = 2 * BINS_DEV
 WCH = 8
+AHEAD = 3
 JOIN = 2
-LAGS = (2, 4, 6)
+LAGS = (3, 6, 9)
 CCH = 128
 MESH = pl.DeviceIdType.MESH
 
@@ -51,8 +54,8 @@
     raws = (raw0, raw1)
     parts_v = lhs.shape[3] // (2 * N_WIN * WCH)
 
-    win_peers = [((xhi + a) % 2) * NZ + (z + b) % NZ for a in range(2) for b in range(NZ)][1:]
-    col_peers = [((y + a) % NY) * 2 + (core + b) % 2 for a in range(NY) for b in range(2)][1:]
+    win_peers = [((xhi + a) % 2) * NZ + (z + b) % NZ for a, b in WIN_STEPS]
+    col_peers = [((y + a) % NY) * 2 + (core + b) % 2 for a, b in COL_STEPS]
     mirror = ((1 - xlo) * N_COL + col, win)
 
     def x_copy(g):
@@ -65,7 +68,7 @@
     partner_copy = pltpu.make_async_copy(partner_hbm, partner, tsem.at[1])
     ids_copy = pltpu.make_async_copy(ids_hbm, block_ids, tsem.at[2])
     table_copy.start()
-    for g in range(chunks):
+    for g in range(AHEAD):
         x_copy(g).start()
     partner_copy.start()
     ids_copy.start()
@@ -110,6 +113,8 @@
 
     def load(g):
         x_copy(g).wait()
+        if g + AHEAD < chunks:
+            x_copy(g + AHEAD).start()
 
     def product_all(g):
         load(g)
@@ -270,23 +275,29 @@
     )(*(pltpu.with_memory_space_constraint(a, pltpu.HBM) for a in (traces, table, partner, block_ids)))
 
 
-def correlate_kernel(scale, lhs, rem, out):
-    k, r = pl.program_id(0), pl.program_id(1)
+def correlate_kernel(scale, lhs, rem, out_hbm, out, sems):
     chunks, n_win = rem.shape[:2]
-    channels = lhs.shape[2]
+    bins, _, channels, _ = lhs.shape
     chans = channels // CCH
     parts_v = chunks // chans
-    columns = []
-    for h in range(chans):
-        rows = [
-            rem[h * parts_v + v, :, r, 2 * k + c].reshape(n_win * WCH, CCH)
-            for c in range(2)
-            for v in range(parts_v)
-        ]
-        columns.append(jnp.concatenate(rows, axis=0))
-    right = jnp.concatenate(columns, axis=1)
-    for t in range(2):
-        out[0, 0, t] = jnp.dot(lhs[k, t], right, preferred_element_type=jnp.float32) * scale
+    copies = []
+    for k in range(bins):
+        for r in range(ROUNDS):
+            columns = []
+            for h in range(chans):
+                rows = [
+                    rem[h * parts_v + v, :, r, 2 * k + c].reshape(n_win * WCH, CCH)
+                    for c in range(2)
+                    for v in range(parts_v)
+                ]
+                columns.append(jnp.concatenate(rows, axis=0))
+            right = jnp.concatenate(columns, axis=1)
+            for t in range(2):
+                out[r, k, t] = jnp.dot(lhs[k, t], right, preferred_element_type=jnp.float32) * scale
+            copies.append(pltpu.make_async_copy(out.at[r, k], out_hbm.at[r, k], sems.at[len(copies)]))
+            copies[-1].start()
+    for copy in copies:
+        copy.wait()
 
 
 def correlate(lhs, rem, scale):
@@ -294,10 +305,10 @@
     out_shape = (ROUNDS, bins, 2, channels, channels)
     return pl.pallas_call(
         functools.partial(correlate_kernel, scale),
-        grid=(bins, ROUNDS),
         out_shape=jax.ShapeDtypeStruct(out_shape, jnp.float32),
         in_specs=[pl.BlockSpec(memory_space=pltpu.VMEM)] * 2,
-        out_specs=pl.BlockSpec((1, 1, 2, channels, channels), lambda k, r: (r, k, 0, 0, 0)),
+        out_specs=pl.BlockSpec(memory_space=pltpu.HBM),
+        scratch_shapes=[pltpu.VMEM(out_shape, jnp.float32), pltpu.SemaphoreType.DMA((bins * ROUNDS,))],
         compiler_params=pltpu.CompilerParams(vmem_limit_bytes=16 * 1024 * 1024),
         name="correlate",
     )(lhs, rem)

time: 62 us -> 55.9 us (0.902)
  Pallas kernels: 61.9 us -> 55.8 us
    pallas_call x1, Pallas kernels: 57.1 us -> 53.4 us  [spread(): pl.pallas_call(spread_kernel, out_shape=(jax.ShapeDtypeStruct(lhs_shape,...]
    pallas_call x1, Pallas kernels: 4.75 us -> 2.38 us  [correlate(): pl.pallas_call(functools.partial(correlate_kernel, scale), out_shape=jax....]
where the time goes in v3:
time: 55.9 us; the launch traced here: 55.8 us
  Pallas kernels  55.8 us (100%)
    pallas_call x1, Pallas kernels, spread(): pl.pallas_call(spread_kernel, out_shape=(jax.ShapeDtypeStruct(lhs_shape,...  53.4 us
    pallas_call x1, Pallas kernels, correlate(): pl.pallas_call(functools.partial(correlate_kernel, scale), out_shape=jax....  2.38 us

profile of v3, /device:TPU:1, one launch (start us, length us, event | category | flops | bytes accessed | tf_op | source)
XLA Modules:
  0.0 55.8 jit_solution(12699593886877378063)
XLA Ops:
  0.0 53.4 %spread.1 = (bf16[4,2,256,512]{3,2,1,0:T(8,128)(2,1)S(1)}, bf16[8,8,2,8,8,128]{5,4,3,2,1,0:T(8,128)(2,1)S(1)}) custom-call(bf16[256,32,1024]{2,1,0:T(8,128)(2,1)} %x_hbm.1, bf16[1024,128]{1,0:T(8,128)(2,1)} %constant.8.table_hbm, s32[2,16]{1,0:T(2,128)} %partner_hbm.1, s32[16]{0:T(128)} %ids_hbm.1), custom_call_target="tpu_custom_call" | custom-call | tf_op jit(solution)/shard_map/spread/pallas_call | solution.py:245
  53.4 2.4 %correlate.1 = f32[2,4,2,256,256]{4,3,2,1,0:T(8,128)} custom-call(bf16[4,2,256,512]{3,2,1,0:T(8,128)(2,1)S(1)} %get-tuple-element.7.lhs, bf16[8,8,2,8,8,128]{5,4,3,2,1,0:T(8,128)(2,1)S(1)} %get-tuple-element.8.rem), custom_call_target="tpu_custom_call" | custom-call | tf_op jit(solution)/shard_map/correlate/pallas_call | solution.py:306

commit v4 on v3

--- a/solution.py
+++ b/solution.py
@@ -42,7 +42,7 @@
 def spread_kernel(
     x_hbm, table_hbm, partner_hbm, ids_hbm, lhs_out, rem_out,
     table, partner, block_ids, raw0, raw1, ybuf, lhs, targets,
-    xsem, tsem, s1, r1, s2, r2, s3, r3, s4, r4, l4, lsem, *buffers,
+    xsem, fsem, tsem, s1, r1, s2, r2, s3, r3, s4, r4, l4, lsem, *buffers,
 ):
     pair = lax.axis_index("pair")
     win = lax.axis_index("win")
@@ -64,11 +64,23 @@
             x_hbm.at[pl.ds(h * CCH, CCH), pl.ds(v * WCH, WCH)], xbufs[g], xsem.at[g]
         )
 
+    blocks = fsem.shape[0]
+    rows = CCH * WCH // blocks
+
+    def first_copy(i):
+        span = CCH // blocks
+        return pltpu.make_async_copy(
+            x_hbm.at[pl.ds(i * span, span), pl.ds(0, WCH)], xbufs[0].at[pl.ds(i * span, span)], fsem.at[i]
+        )
+
     table_copy = pltpu.make_async_copy(table_hbm, table, tsem.at[0])
     partner_copy = pltpu.make_async_copy(partner_hbm, partner, tsem.at[1])
     ids_copy = pltpu.make_async_copy(ids_hbm, block_ids, tsem.at[2])
-    table_copy.start()
-    for g in range(AHEAD):
+    for i in range(blocks):
+        first_copy(i).start()
+        if i == 0:
+            table_copy.start()
+    for g in range(1, AHEAD):
         x_copy(g).start()
     partner_copy.start()
     ids_copy.start()
@@ -99,9 +111,6 @@
             src_ref=src, dst_ref=dst, send_sem=send, recv_sem=recv, device_id=device, device_id_type=MESH
         )
 
-    blocks = 4
-    rows = CCH * WCH // blocks
-
     def product(g, i):
         block = xbufs[g][pl.ds(i * (rows // WCH), rows // WCH)].reshape(rows, SAMPLES)
         raws[g % 2][pl.ds(i * rows, rows), :] = jnp.dot(block, table[...], preferred_element_type=jnp.float32)
@@ -113,15 +122,14 @@
 
     def load(g):
         x_copy(g).wait()
-        if g + AHEAD < chunks:
-            x_copy(g + AHEAD).start()
-
-    def product_all(g):
-        load(g)
-
-        @pl.loop(0, blocks)
-        def _(i):
-            product(g, i)
+        if g + AHEAD - 1 < chunks:
+            x_copy(g + AHEAD - 1).start()
+
+    def product_first():
+        table_copy.wait()
+        for i in range(blocks):
+            first_copy(i).wait()
+            product(0, i)
 
     def whiten_all(g):
         for w in range(WCH):
@@ -138,15 +146,11 @@
 
     def transform(g):
         if g == 0:
-            table_copy.wait()
-            product_all(0)
-            whiten_all(0)
-        elif g == chunks - 1:
+            product_first()
+        if g < chunks - 1:
+            both(g)
+        else:
             whiten_all(g)
-        else:
-            if g == 1:
-                product_all(1)
-            both(g)
         sends[g][...] = ybuf[...].astype(jnp.bfloat16).reshape(N_WIN, PARTS, WCH, CCH)
 
     def phase1(g):
@@ -205,8 +209,8 @@
             if t == 0:
                 pl.semaphore_wait(barrier, len(win_peers) + len(col_peers) + 1)
             phase1(t)
-            if t == 0:
-                find_targets()
+        if t == lag3:
+            find_targets()
         if 0 <= t - lag2 < chunks:
             phase2(t - lag2)
         if 0 <= t - lag3 < chunks:
@@ -256,7 +260,7 @@
             pltpu.VMEM((2 * BINS * WCH, CCH), f32),
             pltpu.VMEM(lhs_shape, bf16),
             pltpu.SMEM((ROUNDS, N_COL), jnp.int32),
-            dma((chunks,)), dma((3,)),
+            dma((chunks,)), dma((4,)), dma((3,)),
             dma((chunks,)), dma((chunks, N_WIN)),
             dma((chunks,)), dma((chunks, N_COL)),
             dma((chunks,)), dma((chunks,)),

time: 55.9 us -> 54.9 us (0.982)
  Pallas kernels: 55.8 us -> 54.8 us
    pallas_call x1, Pallas kernels: 53.4 us -> 52.4 us  [spread(): pl.pallas_call(spread_kernel, out_shape=(jax.ShapeDtypeStruct(lhs_shape,...]
where the time goes in v4:
time: 54.9 us; the launch traced here: 54.8 us
  Pallas kernels  54.8 us (100%)
    pallas_call x1, Pallas kernels, spread(): pl.pallas_call(spread_kernel, out_shape=(jax.ShapeDtypeStruct(lhs_shape,...  52.4 us
    pallas_call x1, Pallas kernels, correlate(): pl.pallas_call(functools.partial(correlate_kernel, scale), out_shape=jax....  2.38 us

profile of v4, /device:TPU:1, one launch (start us, length us, event | category | flops | bytes accessed | tf_op | source)
XLA Modules:
  0.0 54.8 jit_solution(1335388880593551326)
XLA Ops:
  0.0 52.4 %spread.1 = (bf16[4,2,256,512]{3,2,1,0:T(8,128)(2,1)S(1)}, bf16[8,8,2,8,8,128]{5,4,3,2,1,0:T(8,128)(2,1)S(1)}) custom-call(bf16[256,32,1024]{2,1,0:T(8,128)(2,1)} %x_hbm.1, bf16[1024,128]{1,0:T(8,128)(2,1)} %constant.8.table_hbm, s32[2,16]{1,0:T(2,128)} %partner_hbm.1, s32[16]{0:T(128)} %ids_hbm.1), custom_call_target="tpu_custom_call" | custom-call | tf_op jit(solution)/shard_map/spread/pallas_call | solution.py:249
  52.4 2.4 %correlate.1 = f32[2,4,2,256,256]{4,3,2,1,0:T(8,128)} custom-call(bf16[4,2,256,512]{3,2,1,0:T(8,128)(2,1)S(1)} %get-tuple-element.7.lhs, bf16[8,8,2,8,8,128]{5,4,3,2,1,0:T(8,128)(2,1)S(1)} %get-tuple-element.8.rem), custom_call_target="tpu_custom_call" | custom-call | tf_op jit(solution)/shard_map/correlate/pallas_call | solution.py:310

commit v5 on v4

--- a/solution.py
+++ b/solution.py
@@ -25,7 +25,7 @@
 WCH = 8
 AHEAD = 3
 JOIN = 2
-LAGS = (3, 6, 9)
+LAGS = (3, 7, 10)
 CCH = 128
 MESH = pl.DeviceIdType.MESH
 
@@ -159,13 +159,20 @@
         owns[g][win] = sends[g][win]
 
     def phase2(g):
-        for peer in win_peers:
+        def forward(part):
+            @pl.when(part != col)
+            def _():
+                device = (xlo * N_COL + part, win)
+                remote(owns[g].at[part], mids[g].at[pair], s2.at[g], r2.at[g, col], device).start()
+
+            @pl.when(part == col)
+            def _():
+                mids[g][pair] = owns[g][part]
+
+        forward(win)
+        for peer in reversed(win_peers):
             remote(sends[g].at[peer], owns[g].at[peer], s1.at[g], r1.at[g, peer], (pair, peer)).wait_recv()
-        for peer in col_peers:
-            remote(
-                owns[g].at[peer], mids[g].at[pair], s2.at[g], r2.at[g, col], (xlo * N_COL + peer, win)
-            ).start()
-        mids[g][pair] = owns[g][col]
+            forward(peer)
 
     def phase3(g):
         remote(mids[g].at[pair], mids[g].at[pair], s3.at[g], r3.at[g], mirror).start()

time: 54.9 us -> 54.7 us (level)
  no operation moved by 1% of the time
where the time goes in v5:
time: 54.7 us; the launch traced here: 54.6 us
  Pallas kernels  54.6 us (100%)
    pallas_call x1, Pallas kernels, spread(): pl.pallas_call(spread_kernel, out_shape=(jax.ShapeDtypeStruct(lhs_shape,...  52.2 us
    pallas_call x1, Pallas kernels, correlate(): pl.pallas_call(functools.partial(correlate_kernel, scale), out_shape=jax....  2.38 us

profile of v5, /device:TPU:1, one launch (start us, length us, event | category | flops | bytes accessed | tf_op | source)
XLA Modules:
  0.0 54.6 jit_solution(3036755414308295928)
XLA Ops:
  0.0 52.2 %spread.1 = (bf16[4,2,256,512]{3,2,1,0:T(8,128)(2,1)S(1)}, bf16[8,8,2,8,8,128]{5,4,3,2,1,0:T(8,128)(2,1)S(1)}) custom-call(bf16[256,32,1024]{2,1,0:T(8,128)(2,1)} %x_hbm.1, bf16[1024,128]{1,0:T(8,128)(2,1)} %constant.8.table_hbm, s32[2,16]{1,0:T(2,128)} %partner_hbm.1, s32[16]{0:T(128)} %ids_hbm.1), custom_call_target="tpu_custom_call" | custom-call | tf_op jit(solution)/shard_map/spread/pallas_call | solution.py:256
  52.2 2.4 %correlate.1 = f32[2,4,2,256,256]{4,3,2,1,0:T(8,128)} custom-call(bf16[4,2,256,512]{3,2,1,0:T(8,128)(2,1)S(1)} %get-tuple-element.7.lhs, bf16[8,8,2,8,8,128]{5,4,3,2,1,0:T(8,128)(2,1)S(1)} %get-tuple-element.8.rem), custom_call_target="tpu_custom_call" | custom-call | tf_op jit(solution)/shard_map/correlate/pallas_call | solution.py:317

commit v6 on v5

--- a/solution.py
+++ b/solution.py
@@ -25,7 +25,7 @@
 WCH = 8
 AHEAD = 3
 JOIN = 2
-LAGS = (3, 7, 10)
+LAGS = (4, 7, 11)
 CCH = 128
 MESH = pl.DeviceIdType.MESH
 

time: 54.7 us -> 54.6 us (level)
  no operation moved by 1% of the time
where the time goes in v6:
time: 54.6 us; the launch traced here: 54.5 us
  Pallas kernels  54.5 us (100%)
    pallas_call x1, Pallas kernels, spread(): pl.pallas_call(spread_kernel, out_shape=(jax.ShapeDtypeStruct(lhs_shape,...  52.1 us
    pallas_call x1, Pallas kernels, correlate(): pl.pallas_call(functools.partial(correlate_kernel, scale), out_shape=jax....  2.38 us

profile of v6, /device:TPU:1, one launch (start us, length us, event | category | flops | bytes accessed | tf_op | source)
XLA Modules:
  0.0 54.5 jit_solution(3173347970622641907)
XLA Ops:
  0.0 52.1 %spread.1 = (bf16[4,2,256,512]{3,2,1,0:T(8,128)(2,1)S(1)}, bf16[8,8,2,8,8,128]{5,4,3,2,1,0:T(8,128)(2,1)S(1)}) custom-call(bf16[256,32,1024]{2,1,0:T(8,128)(2,1)} %x_hbm.1, bf16[1024,128]{1,0:T(8,128)(2,1)} %constant.8.table_hbm, s32[2,16]{1,0:T(2,128)} %partner_hbm.1, s32[16]{0:T(128)} %ids_hbm.1), custom_call_target="tpu_custom_call" | custom-call | tf_op jit(solution)/shard_map/spread/pallas_call | solution.py:256
  52.1 2.4 %correlate.1 = f32[2,4,2,256,256]{4,3,2,1,0:T(8,128)} custom-call(bf16[4,2,256,512]{3,2,1,0:T(8,128)(2,1)S(1)} %get-tuple-element.7.lhs, bf16[8,8,2,8,8,128]{5,4,3,2,1,0:T(8,128)(2,1)S(1)} %get-tuple-element.8.rem), custom_call_target="tpu_custom_call" | custom-call | tf_op jit(solution)/shard_map/correlate/pallas_call | solution.py:317
